TPU v7x, 512 devices: a whole 4x8x8 slice. The times are simulated.
512 devices in a mesh: prow: 16 (over y, core), pcol: 32 (over z, x).
Axes of the slice: x: 4, y: 8, z: 8, core: 2. Of those that a mesh axis runs over, the one named last changes fastest.
Arguments:
- stiffness: float32 [4, 16, 2, 32, 256, 256], P(None, 'prow', None, 'pcol'), may hold values from -1 to 33, as said below
- pattern: int32 [2, 64], replicated, may hold values 0 or 1
Outputs:
- factored: float32 [4, 16, 2, 32, 256, 256], P(None, 'prow', None, 'pcol')
Inputs may be any that keep to these rules, and one draw needn't show every extreme that they name: `stiffness`: Symmetric; entries off the main diagonal have magnitude at most 1, and the main diagonal's entries lie between 31 and 33.
All inputs are finite; a program needn't handle non-finite values.
Results may differ from a plain program's by a relative error of at most 0.0003.
Values sent between devices are 32-bit elements; how exact they have to be, the bound alone decides.
A program may use at most 64 MiB of HBM per device.

v0:
```python
import jax
import jax.numpy as jnp
from jax import lax
from jax.sharding import PartitionSpec as P


def broadcast(block, axis, source):
    block = jnp.where(lax.axis_index(axis) == source, block, jnp.zeros_like(block))
    return lax.psum(block, axis)


def solve_blocks(factor, blocks):
    count = blocks.shape[0]
    order = blocks.shape[1]
    right_hand = jnp.transpose(blocks, (2, 0, 1)).reshape(order, count * order)
    solved = lax.linalg.triangular_solve(factor, right_hand, left_side=True, lower=True)
    return jnp.transpose(solved.reshape(order, count, order), (1, 2, 0))


def local(stiffness, pattern):
    row_count = stiffness.shape[0]
    col_count = stiffness.shape[2]
    order = stiffness.shape[4]
    nprow = lax.axis_size("prow")
    npcol = lax.axis_size("pcol")
    my_row = lax.axis_index("prow")
    my_col = lax.axis_index("pcol")
    blocks = stiffness.reshape(row_count, col_count, order, order)
    glob_rows = my_row + nprow * jnp.arange(row_count, dtype=jnp.int32)
    glob_cols = my_col + npcol * jnp.arange(col_count, dtype=jnp.int32)
    all_rows = jnp.arange(row_count * nprow, dtype=jnp.int32)
    first_flags = (pattern[0] == 1) & (all_rows > 0)
    second_flags = ((pattern[1] == 1) | first_flags[1] & first_flags) & (all_rows > 1)
    for column, flags in ((0, first_flags), (1, second_flags)):
        local_col = column // npcol
        local_diag = blocks[column // nprow, local_col]
        factor = broadcast(jnp.linalg.cholesky(local_diag), "prow", column % nprow)
        payload = solve_blocks(factor, blocks[:, local_col])
        row_pieces = broadcast(payload, "pcol", column % npcol)
        my_flags = jnp.take(flags, glob_rows)
        panel_blocks = jnp.where(my_flags[:, None, None], row_pieces, jnp.zeros_like(row_pieces))
        source_rows = glob_cols // nprow
        column_pieces = broadcast(
            jnp.take(panel_blocks, source_rows, axis=0), "prow", my_col % nprow
        )
        update = jnp.einsum(
            "iab,jcb->ijac", panel_blocks, column_pieces, precision=lax.Precision.HIGHEST
        )
        keep_mask = (glob_cols[None, :] > column) & (glob_cols[None, :] <= glob_rows[:, None])
        blocks = blocks - jnp.where(keep_mask[:, :, None, None], update, jnp.zeros_like(update))
        old_column = blocks[:, local_col]
        new_column = jnp.where((glob_rows > column)[:, None, None], panel_blocks, old_column)
        new_column = jnp.where((glob_rows == column)[:, None, None], factor[None, :, :], new_column)
        is_panel_col = my_col == column % npcol
        blocks = blocks.at[:, local_col].set(jnp.where(is_panel_col, new_column, old_column))
    return blocks.reshape(stiffness.shape)


def solution(mesh):
    placed = (P(None, "prow", None, "pcol", None, None), P())
    return jax.shard_map(
        local,
        mesh=mesh,
        in_specs=placed,
        out_specs=P(None, "prow", None, "pcol", None, None),
        check_vma=False,
    )
```

profile of v0, /device:TPU:1, one launch (start us, length us, event | category | flops | bytes accessed | tf_op | source)
XLA Modules:
  0.0 959.3 jit_solution(15155828020917416587)
XLA Ops:
  6.5 1.9 copy.15
  8.7 11.7 %cholesky.130 = f32[128,128]{1,0:T(8,128)S(1)} custom-call(f32[128,128]{1,0:T(8,128)S(1)} %cholesky.194), custom_call_target="Cholesky" | custom-call | tf_op jit(solution)/shard_map/jit(cholesky)/cholesky | solution.py:37
  20.5 9.8 %custom-call.13 = f32[1,128,128]{1,2,0:T(8,128)S(1)} custom-call(f32[1,128,128]{2,1,0:T(8,128)S(1)} %get-tuple-element.76), custom_call_target="InvertDiagBlocksLowerTriangular" | custom-call | tf_op jit(solution)/shard_map/jit(cholesky)/cholesky | solution.py:37
  30.8 11.7 %cholesky.147 = f32[128,128]{1,0:T(8,128)S(1)} custom-call(f32[128,128]{1,0:T(8,128)S(1)} %convolution_subtract_fusion.3), custom_call_target="Cholesky" | custom-call | tf_op jit(solution)/shard_map/jit(cholesky)/cholesky | solution.py:37
  45.3 12.5 %all-reduce.10.cloned.1.call-start = ((), (), s32[]{:S(2)}) async-start(), calls=%async_computation.1 | async-start | bytes 2097152 | tf_op jit(solution)/shard_map/psum | solution.py:9
  58.9 1.6 copy.17
  60.5 104.2 %all-reduce.8.cloned.1.call-done = f32[256,256]{1,0:T(8,128)} async-done(((f32[256,256]{1,0:T(8,128)}), f32[256,256]{1,0:T(8,128)}) %all-reduce.8.cloned.1.call-update) | async-done | bytes 262160 | tf_op jit(solution)/shard_map/psum | solution.py:9
  165.8 4.1 while.6
  166.4 1.4 bitcast_dynamic-update-slice_fusion.6
  168.5 1.4 bitcast_dynamic-update-slice_fusion.6
  170.6 20.5 %custom-call.14 = f32[2,128,128]{1,2,0:T(8,128)S(1)} custom-call(f32[2,128,128]{2,1,0:T(8,128)} %copy-done.5), custom_call_target="InvertDiagBlocksLowerTriangular" | custom-call | tf_op jit(solution)/shard_map/triangular_solve/custom-call.0 | solution.py:16
  194.8 2.6 copy.19
  198.3 156.5 %all-reduce.10.cloned.1.call-done = f32[4,256,256]{1,2,0:T(8,128)} async-done(((f32[4,256,256]{1,2,0:T(8,128)}), f32[4,256,256]{1,2,0:T(8,128)}) %all-reduce.10.cloned.1.call-update) | async-done | bytes 1048592 | tf_op jit(solution)/shard_map/psum | solution.py:9
  357.6 1.9 select_select_fusion.2
  360.8 115.4 %all-reduce.12.cloned.1.call-done = f32[2,256,256]{1,2,0:T(8,128)} async-done(((f32[2,256,256]{1,2,0:T(8,128)}), f32[2,256,256]{1,2,0:T(8,128)}) %all-reduce.12.cloned.1.call-update) | async-done | bytes 524304 | tf_op jit(solution)/shard_map/psum | solution.py:9
  476.2 3.2 fusion.1
  481.2 11.7 %cholesky.164 = f32[128,128]{1,0:T(8,128)S(1)} custom-call(f32[128,128]{1,0:T(8,128)S(1)} %cholesky.197), custom_call_target="Cholesky" | custom-call | tf_op jit(solution)/shard_map/jit(cholesky)/cholesky | solution.py:37
  493.6 9.8 %custom-call.15 = f32[1,128,128]{1,2,0:T(8,128)S(1)} custom-call(f32[1,128,128]{2,1,0:T(8,128)S(1)} %get-tuple-element.72), custom_call_target="InvertDiagBlocksLowerTriangular" | custom-call | tf_op jit(solution)/shard_map/jit(cholesky)/cholesky | solution.py:37
  504.0 11.9 %cholesky.181 = f32[128,128]{1,0:T(8,128)S(1)} custom-call(f32[128,128]{1,0:T(8,128)S(1)} %convolution_subtract_fusion.2), custom_call_target="Cholesky" | custom-call | tf_op jit(solution)/shard_map/jit(cholesky)/cholesky | solution.py:37
  518.9 114.4 %all-reduce.14.cloned.1.call-done = f32[256,256]{1,0:T(8,128)} async-done(((f32[256,256]{1,0:T(8,128)}), f32[256,256]{1,0:T(8,128)}) %all-reduce.14.cloned.1.call-update) | async-done | bytes 262160 | tf_op jit(solution)/shard_map/psum | solution.py:9
  634.3 4.1 while.7
  634.9 1.4 bitcast_dynamic-update-slice_fusion.7
  636.9 1.4 bitcast_dynamic-update-slice_fusion.7
  638.4 19.7 %custom-call.16 = f32[2,128,128]{1,2,0:T(8,128)S(1)} custom-call(f32[2,128,128]{2,1,0:T(8,128)S(1)} %get-tuple-element.48), custom_call_target="InvertDiagBlocksLowerTriangular" | custom-call | tf_op jit(solution)/shard_map/triangular_solve/custom-call.0 | solution.py:16
  661.8 2.6 copy.27
  666.4 155.4 %all-reduce.16.cloned.1.call-done = f32[4,256,256]{1,2,0:T(8,128)} async-done(((f32[4,256,256]{1,2,0:T(8,128)}), f32[4,256,256]{1,2,0:T(8,128)}) %all-reduce.16.cloned.1.call-update) | async-done | bytes 1048592 | tf_op jit(solution)/shard_map/psum | solution.py:9
  821.8 2.4 broadcast_select_fusion
  824.2 2.6 gather_fusion.3
  826.8 2.0 select_select_fusion.1
  829.1 116.4 %all-reduce.18.cloned.1.call-done = f32[2,256,256]{1,2,0:T(8,128)} async-done(((f32[2,256,256]{1,2,0:T(8,128)}), f32[2,256,256]{1,2,0:T(8,128)}) %all-reduce.18.cloned.1.call-update) | async-done | bytes 524304 | tf_op jit(solution)/shard_map/psum | solution.py:9
  945.5 3.4 fusion
  950.3 1.8 copy.32
  (100 shorter events, 28.9 us)
Async XLA Ops:
  6.5 158.2 %all-reduce.8.cloned.1.call-start = ((), (), s32[]{:S(2)}) async-start(), calls=%async_computation | async-start | bytes 524288 | tf_op jit(solution)/shard_map/psum | solution.py:9
  8.7 50.3 %copy-start.6 = (s32[2,64]{1,0:T(2,128)S(1)}, s32[2,64]{1,0:T(2,128)}, u32[]{:S(2)}) copy-start(s32[2,64]{1,0:T(2,128)} %param.14) | copy-start | bytes 1540
  45.3 309.5 %all-reduce.10.cloned.1.call-start = ((), (), s32[]{:S(2)}) async-start(), calls=%async_computation.1 | async-start | bytes 2097152 | tf_op jit(solution)/shard_map/psum | solution.py:9
  169.9 0.7 copy-start.5
  197.4 278.8 %all-reduce.12.cloned.1.call-start = ((), (), s32[]{:S(2)}) async-start(), calls=%async_computation.2 | async-start | bytes 1048576 | tf_op jit(solution)/shard_map/psum | solution.py:9
  359.5 273.8 %all-reduce.14.cloned.1.call-start = ((), (), s32[]{:S(2)}) async-start(), calls=%async_computation.3 | async-start | bytes 524288 | tf_op jit(solution)/shard_map/psum | solution.py:9
  476.2 4.5 copy-start.2
  479.4 1.3 copy-start
  518.5 303.2 %all-reduce.16.cloned.1.call-start = ((), (), s32[]{:S(2)}) async-start(), calls=%async_computation.4 | async-start | bytes 2097152 | tf_op jit(solution)/shard_map/psum | solution.py:9
  664.4 281.1 %all-reduce.18.cloned.1.call-start = ((), (), s32[]{:S(2)}) async-start(), calls=%async_computation.5 | async-start | bytes 1048576 | tf_op jit(solution)/shard_map/psum | solution.py:9
  666.3 162.5 %copy-start.1 = (f32[4,2,256,256]{2,3,0,1:T(8,128)S(1)}, f32[4,2,256,256]{2,3,0,1:T(8,128)}, u32[]{:S(2)}) copy-start(f32[4,2,256,256]{2,3,0,1:T(8,128)} %copy-done) | copy-start | bytes 6291460
  826.8 2.1 copy-start.4
  948.9 1.2 copy-start.3
Sparse Core Ops, SparseCore 0:
  45.5 119.2 all-reduce.7
  197.6 157.2 all-reduce.9
  359.7 116.4 all-reduce.11
  518.6 114.6 all-reduce.13
  664.5 157.1 all-reduce.15
  828.9 116.4 all-reduce.17
where the time goes:
time: 968 us; the launch traced here: 959 us
  waiting for transfers between devices  763 us (79%)
  other arithmetic  122 us (13%)
  local copies, waits for them, and re-layouts  33.3 us (3%)
  between operations  16.9 us (2%)
  starting transfers between devices  12.7 us (1%)
  matrix products  12 us (1%)
    psum x6, waiting for transfers between devices, broadcast(): return lax.psum(block, axis)  762 us
    another operation x13, other arithmetic, local(): factor = broadcast(jnp.linalg.cholesky(local_diag), 'prow', column % nprow)  68.9 us
    another operation x5, other arithmetic, solve_blocks(): lax.linalg.triangular_solve(factor, right_hand, left_side=True, lower=True)  42.1 us
  transfers between devices with their start and end apart: 6, of which 6 were waited for; matrix products, arithmetic and copies ran while one was open for 1% of the time, Pallas kernels for 0%

commit v1 on v0

--- a/solution.py
+++ b/solution.py
@@ -6,7 +6,7 @@
 
 def broadcast(block, axis, source):
     block = jnp.where(lax.axis_index(axis) == source, block, jnp.zeros_like(block))
-    return lax.psum(block, axis)
+    return jnp.sum(lax.all_gather(block, axis), axis=0)
 
 
 def solve_blocks(factor, blocks):

time: 968 us -> 913 us (0.943)
  waiting for transfers between devices: 763 us -> 671 us
  other arithmetic: 122 us -> 161 us
  starting transfers between devices: 12.7 us -> 0.85 us
    psum x6 -> x0, waiting for transfers between devices: 762 us -> none  [broadcast(): return lax.psum(block, axis)]
    all_gather x0 -> x6, waiting for transfers between devices: none -> 671 us  [broadcast(): return jnp.sum(lax.all_gather(block, axis), axis=0)]
    reduce_sum x0 -> x6, other arithmetic: none -> 39.5 us  [broadcast(): return jnp.sum(lax.all_gather(block, axis), axis=0)]
    psum x6 -> x0, starting transfers between devices: 12.7 us -> none  [broadcast(): return lax.psum(block, axis)]
where the time goes in v1:
time: 913 us; the launch traced here: 905 us
  waiting for transfers between devices  671 us (73%)
  other arithmetic  161 us (18%)
  local copies, waits for them, and re-layouts  40.8 us (4%)
  between operations  16.7 us (2%)
  matrix products  14.8 us (2%)
    all_gather x6, waiting for transfers between devices, broadcast(): return jnp.sum(lax.all_gather(block, axis), axis=0)  671 us
    another operation x13, other arithmetic, local(): factor = broadcast(jnp.linalg.cholesky(local_diag), 'prow', column % nprow)  69.9 us
    another operation x5, other arithmetic, solve_blocks(): lax.linalg.triangular_solve(factor, right_hand, left_side=True, lower=True)  40.9 us
    reduce_sum x6, other arithmetic, broadcast(): return jnp.sum(lax.all_gather(block, axis), axis=0)  39.5 us
  transfers between devices with their start and end apart: 6, of which 6 were waited for; matrix products, arithmetic and copies ran while one was open for 1% of the time, Pallas kernels for 0%

profile of v1, /device:TPU:1, one launch (start us, length us, event | category | flops | bytes accessed | tf_op | source)
XLA Modules:
  0.0 904.5 jit_solution(850210557994261556)
XLA Ops:
  6.5 1.9 copy.35
  8.7 11.7 %cholesky.130 = f32[128,128]{1,0:T(8,128)S(1)} custom-call(f32[128,128]{1,0:T(8,128)S(1)} %cholesky.194), custom_call_target="Cholesky" | custom-call | tf_op jit(solution)/shard_map/jit(cholesky)/cholesky | solution.py:37
  20.5 9.8 %custom-call.13 = f32[1,128,128]{1,2,0:T(8,128)S(1)} custom-call(f32[1,128,128]{2,1,0:T(8,128)S(1)} %get-tuple-element.78), custom_call_target="InvertDiagBlocksLowerTriangular" | custom-call | tf_op jit(solution)/shard_map/jit(cholesky)/cholesky | solution.py:37
  30.8 11.7 %cholesky.147 = f32[128,128]{1,0:T(8,128)S(1)} custom-call(f32[128,128]{1,0:T(8,128)S(1)} %convolution_subtract_fusion.3), custom_call_target="Cholesky" | custom-call | tf_op jit(solution)/shard_map/jit(cholesky)/cholesky | solution.py:37
  48.6 47.2 %all-gather.13.cloned.1.call-done = f32[4096,256]{1,0:T(8,128)} async-done(((f32[256,256]{1,0:T(8,128)}), f32[4096,256]{1,0:T(8,128)}) %all-gather.13.cloned.1.call-update) | async-done | bytes 4194320 | tf_op jit(solution)/shard_map/all_gather | solution.py:9
  95.9 2.5 reduce_sum.58
  98.5 3.9 while.6
  102.9 19.7 %custom-call.14 = f32[2,128,128]{1,2,0:T(8,128)S(1)} custom-call(f32[2,128,128]{2,1,0:T(8,128)S(1)} %get-tuple-element.47), custom_call_target="InvertDiagBlocksLowerTriangular" | custom-call | tf_op jit(solution)/shard_map/triangular_solve/custom-call.0 | solution.py:16
  126.8 237.3 %all-gather.15.cloned.1.call-done = f32[128,256,256]{2,1,0:T(8,128)} async-done(((f32[4,256,256]{2,1,0:T(8,128)}), f32[128,256,256]{2,1,0:T(8,128)}) %all-gather.15.cloned.1.call-update) | async-done | bytes 33554448 | tf_op jit(solution)/shard_map/all_gather | solution.py:9
  364.1 12.0 %reduce_sum.59 = f32[4,256,256]{2,1,0:T(8,128)S(1)} reduce(f32[32,4,256,256]{3,2,1,0:T(8,128)} %bitcast.160, f32[]{:T(128)} %constant.175.clone.1), dimensions={0}, to_apply=%region_5.9 | reduce | flops 8126464 | bytes 34603012 | tf_op jit(solution)/shard_map/reduce_sum | solution.py:9
  381.1 54.8 %all-gather.17.cloned.1.call-done = f32[32,256,256]{2,1,0:T(8,128)} async-done(((f32[2,256,256]{2,1,0:T(8,128)}), f32[32,256,256]{2,1,0:T(8,128)}) %all-gather.17.cloned.1.call-update) | async-done | bytes 8388624 | tf_op jit(solution)/shard_map/all_gather | solution.py:9
  435.8 4.8 reduce_sum.60
  440.6 4.0 fusion.1
  450.7 11.7 %cholesky.164 = f32[128,128]{1,0:T(8,128)S(1)} custom-call(f32[128,128]{1,0:T(8,128)S(1)} %cholesky.197), custom_call_target="Cholesky" | custom-call | tf_op jit(solution)/shard_map/jit(cholesky)/cholesky | solution.py:37
  462.9 9.8 %custom-call.15 = f32[1,128,128]{1,2,0:T(8,128)S(1)} custom-call(f32[1,128,128]{2,1,0:T(8,128)S(1)} %get-tuple-element.74), custom_call_target="InvertDiagBlocksLowerTriangular" | custom-call | tf_op jit(solution)/shard_map/jit(cholesky)/cholesky | solution.py:37
  474.9 11.9 %cholesky.181 = f32[128,128]{1,0:T(8,128)S(1)} custom-call(f32[128,128]{1,0:T(8,128)S(1)} %convolution_subtract_fusion.2), custom_call_target="Cholesky" | custom-call | tf_op jit(solution)/shard_map/jit(cholesky)/cholesky | solution.py:37
  494.1 40.3 %all-gather.19.cloned.1.call-done = f32[4096,256]{1,0:T(8,128)} async-done(((f32[256,256]{1,0:T(8,128)}), f32[4096,256]{1,0:T(8,128)}) %all-gather.19.cloned.1.call-update) | async-done | bytes 4194320 | tf_op jit(solution)/shard_map/all_gather | solution.py:9
  534.4 2.6 reduce_sum.62
  537.7 6.7 while.7
  539.0 2.2 bitcast_dynamic-update-slice_fusion.6
  542.4 2.1 bitcast_dynamic-update-slice_fusion.6
  545.1 20.5 %custom-call.16 = f32[2,128,128]{1,2,0:T(8,128)S(1)} custom-call(f32[2,128,128]{2,1,0:T(8,128)} %copy-done.7), custom_call_target="InvertDiagBlocksLowerTriangular" | custom-call | tf_op jit(solution)/shard_map/triangular_solve/custom-call.0 | solution.py:16
  566.3 1.7 convolution_subtract_fusion
  572.0 236.2 %all-gather.21.cloned.1.call-done = f32[128,256,256]{2,1,0:T(8,128)} async-done(((f32[4,256,256]{2,1,0:T(8,128)}), f32[128,256,256]{2,1,0:T(8,128)}) %all-gather.21.cloned.1.call-update) | async-done | bytes 33554448 | tf_op jit(solution)/shard_map/all_gather | solution.py:9
  808.2 12.9 %reduce_sum.63 = f32[4,256,256]{2,1,0:T(8,128)} reduce(f32[32,4,256,256]{3,2,1,0:T(8,128)} %bitcast.161, f32[]{:T(128)} %constant.175.clone.1), dimensions={0}, to_apply=%region_8.13 | reduce | flops 8126464 | bytes 34603012 | tf_op jit(solution)/shard_map/reduce_sum | solution.py:9
  823.8 2.6 gather_fusion.3
  826.4 1.9 select_select_fusion
  828.3 2.1 copy.56
  831.3 54.9 %all-gather.23.cloned.1.call-done = f32[32,256,256]{2,1,0:T(8,128)} async-done(((f32[2,256,256]{2,1,0:T(8,128)}), f32[32,256,256]{2,1,0:T(8,128)}) %all-gather.23.cloned.1.call-update) | async-done | bytes 8388624 | tf_op jit(solution)/shard_map/all_gather | solution.py:9
  886.2 4.8 reduce_sum.64
  891.0 3.4 fusion
  895.6 1.8 copy.64
  (121 shorter events, 47.0 us)
Async XLA Ops:
  6.5 89.3 %all-gather.13.cloned.1.call-start = ((), (), s32[]{:S(2)}) async-start(), calls=%async_computation | async-start | bytes 4456448 | tf_op jit(solution)/shard_map/all_gather | solution.py:9
  8.5 38.4 %copy-start = (f32[4,1,2,1,256,256]{4,5,2,0,3,1:T(8,128)}, f32[4,1,2,1,256,256]{4,5,2,0,3,1:T(8,128)S(1)}, u32[]{:S(2)}) copy-start(f32[4,1,2,1,256,256]{4,5,2,0,3,1:T(8,128)S(1)} %copy.35) | copy-start | bytes 6291460
  45.3 318.8 %all-gather.15.cloned.1.call-start = ((), (), s32[]{:S(2)}) async-start(), calls=%async_computation.1 | async-start | bytes 34603008 | tf_op jit(solution)/shard_map/all_gather | solution.py:9
  102.4 0.5 copy-start.11
  124.6 1.4 copy-start.9
  125.9 309.9 %all-gather.17.cloned.1.call-start = ((), (), s32[]{:S(2)}) async-start(), calls=%async_computation.2 | async-start | bytes 8912896 | tf_op jit(solution)/shard_map/all_gather | solution.py:9
  376.6 4.5 copy-start.1
  380.1 154.3 %all-gather.19.cloned.1.call-start = ((), (), s32[]{:S(2)}) async-start(), calls=%async_computation.3 | async-start | bytes 4456448 | tf_op jit(solution)/shard_map/all_gather | solution.py:9
  446.2 1.0 copy-start.4
  446.2 44.5 %copy-start.2 = (f32[256,4,256]{2,0,1:T(8,128)S(1)}, f32[256,4,256]{2,0,1:T(8,128)}, u32[]{:S(2)}) copy-start(f32[256,4,256]{2,0,1:T(8,128)} %fusion.8) | copy-start | bytes 3145732
  449.9 0.7 copy-start.6
  490.7 317.5 %all-gather.21.cloned.1.call-start = ((), (), s32[]{:S(2)}) async-start(), calls=%async_computation.4 | async-start | bytes 34603008 | tf_op jit(solution)/shard_map/all_gather | solution.py:9
  534.4 31.2 %copy-start.3 = (f32[256,4,256]{0,2,1:T(8,128)S(1)}, f32[256,4,256]{0,2,1:T(8,128)}, u32[]{:S(2)}) copy-start(f32[256,4,256]{0,2,1:T(8,128)} %copy.51) | copy-start | bytes 3145732
  544.5 0.6 copy-start.7
  568.7 2.0 copy-start.10
  570.0 316.1 %all-gather.23.cloned.1.call-start = ((), (), s32[]{:S(2)}) async-start(), calls=%async_computation.5 | async-start | bytes 8912896 | tf_op jit(solution)/shard_map/all_gather | solution.py:9
  886.2 4.8 copy-start.8
  894.4 1.0 copy-start.5
Sparse Core Ops, SparseCore 0:
  45.4 50.4 all-gather.12
  126.0 237.9 all-gather.14
  380.2 55.5 all-gather.16
  490.8 43.5 all-gather.18
  570.2 237.9 all-gather.20
  830.5 55.5 all-gather.22
